TPU v7x, 512 devices: a whole 4x8x8 slice. The times are simulated.
512 devices in a mesh: centre: 16 (over y, core), sample: 32 (over z, x).
Axes of the slice: x: 4, y: 8, z: 8, core: 2. Of those that a mesh axis runs over, the one named last changes fastest.
Arguments:
- centres: bfloat16 [1024, 32768], P(None, 'centre'), may hold values from -40 to 40
- pool: bfloat16 [1024, 32768], P('centre', 'sample'), may hold values from -40 to 40
- labels: int32 [32768], P('sample'), may hold values from 0 to 143
- picks: int32 [2, 16384], P(None, 'sample'), may hold values from 0 to 32767, as said below
- coefs: float32 [144, 32768], P(None, ('centre', 'sample')), may hold values from -192 to 1024000
Outputs:
- new_coefs: float32 [144, 32768], P(None, ('centre', 'sample'))
Inputs may be any that keep to these rules, and one draw needn't show every extreme that they name: `picks`: entry b of a step's batch is a pool column in [(b // 512) * 1024, (b // 512 + 1) * 1024); entries may repeat.
All inputs are finite; a program needn't handle non-finite values.
Results may differ from a plain program's by a relative error of at most 0.00065.
Values may be sent and summed in bfloat16 or wider, within the bound.
No kernel may reach another device: no remote copies, remote signals or barrier semaphores. Data moves between devices by JAX's collectives and lax.ppermute only.
A program may use at most 64 MiB of HBM per device.

v0:
```python
import jax
import jax.numpy as jnp
from jax import lax
from jax.sharding import PartitionSpec as P

STEPS = 2
LOGIT_GAIN = 16.0
LENGTH_SCALE = 0.5
STEP_GAIN = 2048.0
EPS = 1e-06


def from_everyone(array, axis):
    peers = lax.axis_size(axis)
    return lax.all_to_all(
        jnp.broadcast_to(array[None], (peers, *array.shape)), axis, 0, 0, tiled=True
    )


def joined_along(parts, dim):
    dims = list(parts.shape[1:])
    dims[dim] *= parts.shape[0]
    return jnp.moveaxis(parts, 0, dim).reshape(dims)


def collect(array, axis, dim):
    parts = from_everyone(array, axis)
    return joined_along(parts, dim)


def over_pieces(array, axis):
    return lax.all_gather(array, axis).sum(0)


def cut_along(array, dim, peers):
    dims = array.shape
    parts = array.reshape(*dims[:dim], peers, dims[dim] // peers, *dims[dim + 1 :])
    return jnp.moveaxis(parts, dim, 0)


def summed_on_arrival(array, axis, dim):
    peers = lax.axis_size(axis)
    parts = lax.all_to_all(cut_along(array, dim, peers), axis, 0, 0, tiled=True)
    return jnp.sum(parts, axis=0)


def laplace(cross, sample_sq, centre_sq, width):
    mean_sq = (sample_sq[:, None] + centre_sq[None, :] - 2.0 * cross) / width
    return jnp.exp(-jnp.sqrt(mean_sq + EPS) / LENGTH_SCALE).astype(jnp.bfloat16)


def on_device(centres, pool, labels, picks, coefs):
    width = centres.shape[0]
    cen_dev = centres.shape[1]
    pool_dev = pool.shape[1]
    batch_dev = picks.shape[1]
    classes = coefs.shape[0]
    total_centres = cen_dev * lax.axis_size("centre")
    total_batch = batch_dev * lax.axis_size("sample")
    rate = STEP_GAIN * LOGIT_GAIN / total_batch
    centre_sq = jnp.sum(jnp.square(centres.astype(jnp.float32)), axis=0)
    local_picks = picks - lax.axis_index("sample") * pool_dev
    current = coefs
    for step in range(STEPS):
        coef_half = collect(current.astype(jnp.bfloat16), "sample", 1)
        chosen = local_picks[step]
        feats = jnp.take(pool, chosen, axis=1)
        labs = jnp.take(labels, chosen)
        gathered = lax.all_gather(feats, "centre", axis=0, tiled=True)
        cross = lax.dot_general(
            gathered, centres, (((0,), (0,)), ((), ())), preferred_element_type=jnp.float32
        )
        sample_sq = jnp.sum(jnp.square(gathered.astype(jnp.float32)), axis=0)
        kern = laplace(cross, sample_sq, centre_sq, width)
        partial_logits = lax.dot_general(
            coef_half, kern, (((1,), (1,)), ((), ())), preferred_element_type=jnp.float32
        )
        logits = over_pieces(partial_logits, "centre") * (LOGIT_GAIN / total_centres)
        top = jnp.max(logits, axis=0, keepdims=True)
        expo = jnp.exp(logits - top)
        probs = expo / jnp.sum(expo, axis=0, keepdims=True)
        class_ids = jnp.arange(classes, dtype=jnp.int32)
        onehot = (class_ids[:, None] == labs[None, :]).astype(jnp.float32)
        resid = (probs - onehot).astype(jnp.bfloat16)
        grad_part = jnp.dot(resid, kern, preferred_element_type=jnp.float32)
        current = current - rate * summed_on_arrival(grad_part, "sample", 1)
    return current


def solution(mesh):
    placed = (
        P(None, "centre"),
        P("centre", "sample"),
        P("sample"),
        P(None, "sample"),
        P(None, ("centre", "sample")),
    )
    return jax.shard_map(
        on_device,
        mesh=mesh,
        in_specs=placed,
        out_specs=P(None, ("centre", "sample")),
        check_vma=False,
    )
```

profile of v0, /device:TPU:2, one launch (start us, length us, event | category | flops | bytes accessed | tf_op | source)
XLA Modules:
  0.0 336.5 jit_solution(12417494301291164431)
XLA Ops:
  7.3 2.3 gather_fusion.1
  9.6 1.1 copy.40
  10.7 1.3 gather_fusion
  12.9 0.8 convert_element_type.36
  13.8 1.2 broadcast_in_dim.19
  14.9 13.5 %all-to-all-start = ((bf16[32,144,64]{1,2,0:T(8,128)(2,1)}), bf16[32,144,64]{1,2,0:T(8,128)(2,1)S(1)}, u32[]{:S(2)}, u32[]{:S(2)}) async-start(bf16[32,144,64]{1,2,0:T(8,128)(2,1)} %broadcast_in_dim.19), calls=%async_computation | async-start | bytes 2097152 | tf_op jit(solution)/shard_map/all_to_all | solution.py:15
  28.4 3.1 multiply_reduce_fusion
  31.5 27.1 %all-gather.7.cloned.1.call-done = bf16[1024,512]{1,0:T(8,128)(2,1)} async-done(((bf16[64,512]{1,0:T(8,128)(2,1)}), bf16[1024,512]{1,0:T(8,128)(2,1)}) %all-gather.7.cloned.1.call-update) | async-done | bytes 1048592 | tf_op jit(solution)/shard_map/all_gather | solution.py:69
  58.6 1.5 multiply_reduce_fusion.2
  60.1 6.8 %exponential_convert_fusion.1 = bf16[512,2048]{1,0:T(8,128)(2,1)S(1)} fusion(bf16[1024,512]{1,0:T(8,128)(2,1)} %all-gather.7.cloned.1.call-done, bf16[1024,2048]{1,0:T(8,128)(2,1)} %param.9, f32[2048]{0:T(1024)S(1)} %multiply_reduce_fusion, f32[512]{0:T(512)S(1)} %multiply_reduce_fusion.2), kind=kOutput, calls=%fused_computation.6 | convolution fusion | flops 2155872256 | bytes 7350272 | tf_op jit(solution)/shard_map/dot_general | solution.py:70
  66.9 1.6 convolution_bitcast_fusion
  68.4 44.5 %all-gather.11.cloned.1.call-done = f32[2304,512]{1,0:T(8,128)} async-done(((f32[144,512]{1,0:T(8,128)}), f32[2304,512]{1,0:T(8,128)}) %all-gather.11.cloned.1.call-update) | async-done | bytes 4718608 | tf_op jit(solution)/shard_map/all_gather | solution.py:32
  113.0 2.9 reduce_sum.83
  116.0 1.6 fusion.2
  117.5 2.1 reshape.34
  119.6 2.4 copy.43
  122.0 10.6 %all-to-all-start.1 = ((f32[32,144,64]{1,2,0:T(8,128)}), f32[32,144,64]{1,2,0:T(8,128)S(1)}, u32[]{:S(2)}, u32[]{:S(2)}) async-start(f32[32,144,64]{1,2,0:T(8,128)} %copy.43), calls=%async_computation.1 | async-start | bytes 4194304 | tf_op jit(solution)/shard_map/all_to_all | solution.py:43
  132.7 2.3 gather_fusion.3
  135.0 1.3 gather_fusion.2
  137.3 45.0 %all-to-all-done.1 = f32[32,144,64]{1,2,0:T(8,128)S(1)} async-done(((f32[32,144,64]{1,2,0:T(8,128)}), f32[32,144,64]{1,2,0:T(8,128)S(1)}, u32[]{:S(2)}, u32[]{:S(2)}) %all-to-all-start.1) | async-done | bytes 1179680 | tf_op jit(solution)/shard_map/all_to_all | solution.py:43
  182.5 1.1 broadcast_in_dim.20
  183.6 6.5 %all-to-all-start.2 = ((bf16[32,144,64]{1,2,0:T(8,128)(2,1)}), bf16[32,144,64]{1,2,0:T(8,128)(2,1)S(1)}, u32[]{:S(2)}, u32[]{:S(2)}) async-start(bf16[32,144,64]{1,2,0:T(8,128)(2,1)} %broadcast_in_dim.20), calls=%async_computation.2 | async-start | bytes 2097152 | tf_op jit(solution)/shard_map/all_to_all | solution.py:15
  190.2 1.5 multiply_reduce_fusion.1
  191.7 6.7 %exponential_convert_fusion = bf16[512,2048]{1,0:T(8,128)(2,1)S(1)} fusion(bf16[1024,512]{1,0:T(8,128)(2,1)} %all-gather.9.cloned.1.call-done, bf16[1024,2048]{1,0:T(8,128)(2,1)} %param.9, f32[512]{0:T(512)S(1)} %multiply_reduce_fusion.1, f32[2048]{0:T(1024)S(1)} %multiply_reduce_fusion), kind=kOutput, calls=%fused_computation.5 | convolution fusion | flops 2155872256 | bytes 7350272 | tf_op jit(solution)/shard_map/dot_general | solution.py:70
  198.4 19.8 %all-to-all-done.2 = bf16[32,144,64]{1,2,0:T(8,128)(2,1)S(1)} async-done(((bf16[32,144,64]{1,2,0:T(8,128)(2,1)}), bf16[32,144,64]{1,2,0:T(8,128)(2,1)S(1)}, u32[]{:S(2)}, u32[]{:S(2)}) %all-to-all-start.2) | async-done | bytes 589856 | tf_op jit(solution)/shard_map/all_to_all | solution.py:15
  218.2 1.6 fusion.16
  219.8 39.4 %all-gather.13.cloned.1.call-done = f32[2304,512]{1,0:T(8,128)} async-done(((f32[144,512]{1,0:T(8,128)}), f32[2304,512]{1,0:T(8,128)}) %all-gather.13.cloned.1.call-update) | async-done | bytes 4718608 | tf_op jit(solution)/shard_map/all_gather | solution.py:32
  259.2 2.9 reduce_sum.87
  262.1 2.1 fusion.3
  264.3 0.9 reshape.36
  265.2 2.4 copy.49
  267.6 61.6 %all_to_all.20 = f32[32,144,64]{1,2,0:T(8,128)S(1)} all-to-all(f32[32,144,64]{1,2,0:T(8,128)} %copy.49), channel_id=1, replica_groups=mesh['centre'=16,'sample'=32] {'sample'}, dimensions={0} | all-to-all | bytes 2359296 | tf_op jit(solution)/shard_map/all_to_all | solution.py:43
  (42 shorter events, 3.9 us)
Async XLA Ops:
  6.5 0.7 copy-start
  6.5 52.0 %all-gather.7.cloned.1.call-start = ((), (), s32[]{:S(2)}) async-start(), calls=%async_computation.4 | async-start | bytes 1114112 | tf_op jit(solution)/shard_map/all_gather | solution.py:69
  14.9 51.9 %all-to-all-start = ((bf16[32,144,64]{1,2,0:T(8,128)(2,1)}), bf16[32,144,64]{1,2,0:T(8,128)(2,1)S(1)}, u32[]{:S(2)}, u32[]{:S(2)}) async-start(bf16[32,144,64]{1,2,0:T(8,128)(2,1)} %broadcast_in_dim.19), calls=%async_computation | async-start | bytes 2097152 | tf_op jit(solution)/shard_map/all_to_all | solution.py:15
  28.4 84.6 %all-gather.11.cloned.1.call-start = ((), (), s32[]{:S(2)}) async-start(), calls=%async_computation.6 | async-start | bytes 5013504 | tf_op jit(solution)/shard_map/all_gather | solution.py:32
  122.0 60.4 %copy-start.4 = (f32[144,64]{0,1:T(8,128)S(1)}, f32[144,64]{0,1:T(8,128)}, u32[]{:S(2)}) copy-start(f32[144,64]{0,1:T(8,128)} %param.13) | copy-start | bytes 110596
  122.0 60.3 %all-to-all-start.1 = ((f32[32,144,64]{1,2,0:T(8,128)}), f32[32,144,64]{1,2,0:T(8,128)S(1)}, u32[]{:S(2)}, u32[]{:S(2)}) async-start(f32[32,144,64]{1,2,0:T(8,128)} %copy.43), calls=%async_computation.1 | async-start | bytes 4194304 | tf_op jit(solution)/shard_map/all_to_all | solution.py:43
  132.7 57.5 %all-gather.9.cloned.1.call-start = ((), (), s32[]{:S(2)}) async-start(), calls=%async_computation.5 | async-start | bytes 1114112 | tf_op jit(solution)/shard_map/all_gather | solution.py:69
  182.5 7.7 %copy-start.2 = (f32[144,64]{0,1:T(8,128)}, f32[144,64]{0,1:T(8,128)S(1)}, u32[]{:S(2)}) copy-start(f32[144,64]{0,1:T(8,128)S(1)} %reduce_sum.85) | copy-start | bytes 110596
  183.6 34.6 %all-to-all-start.2 = ((bf16[32,144,64]{1,2,0:T(8,128)(2,1)}), bf16[32,144,64]{1,2,0:T(8,128)(2,1)S(1)}, u32[]{:S(2)}, u32[]{:S(2)}) async-start(bf16[32,144,64]{1,2,0:T(8,128)(2,1)} %broadcast_in_dim.20), calls=%async_computation.2 | async-start | bytes 2097152 | tf_op jit(solution)/shard_map/all_to_all | solution.py:15
  190.1 69.1 %all-gather.13.cloned.1.call-start = ((), (), s32[]{:S(2)}) async-start(), calls=%async_computation.7 | async-start | bytes 5013504 | tf_op jit(solution)/shard_map/all_gather | solution.py:32
  198.4 60.7 %copy-start.1 = (bf16[512,2048]{1,0:T(8,128)(2,1)}, bf16[512,2048]{1,0:T(8,128)(2,1)S(1)}, u32[]{:S(2)}) copy-start(bf16[512,2048]{1,0:T(8,128)(2,1)S(1)} %exponential_convert_fusion) | copy-start | bytes 6291460
  267.6 61.7 %copy-start.3 = (f32[144,64]{0,1:T(8,128)S(1)}, f32[144,64]{0,1:T(8,128)}, u32[]{:S(2)}) copy-start(f32[144,64]{0,1:T(8,128)} %copy-done.2) | copy-start | bytes 110596
  267.6 61.7 %copy-start.5 = (f32[144,64]{0,1:T(8,128)S(1)}, f32[144,64]{0,1:T(8,128)}, u32[]{:S(2)}) copy-start(f32[144,64]{0,1:T(8,128)} %param.13) | copy-start | bytes 110596
Sparse Core Ops, SparseCore 0:
  13.0 45.5 all-gather.6
  68.6 44.3 all-gather.10
  137.4 38.9 all-gather.8
  219.9 39.2 all-gather.12
where the time goes:
time: 337 us
  waiting for transfers between devices  176 us (52%)
  blocking collectives  61.6 us (18%)
  starting transfers between devices  30.7 us (9%)
  matrix products  20.3 us (6%)
  local copies, waits for them, and re-layouts  19.9 us (6%)
  other arithmetic  14.8 us (4%)
  between operations  13.4 us (4%)
    all_gather x2, waiting for transfers between devices, over_pieces(): return lax.all_gather(array, axis).sum(0)  83.9 us
    all_to_all x1, blocking collectives, summed_on_arrival(): parts = lax.all_to_all(cut_along(array, dim, peers), axis, 0, 0, tiled=True)  61.6 us
    all_to_all x1, waiting for transfers between devices, summed_on_arrival(): parts = lax.all_to_all(cut_along(array, dim, peers), axis, 0, 0, tiled=True)  45 us
    all_gather x2, waiting for transfers between devices, on_device(): gathered = lax.all_gather(feats, 'centre', axis=0, tiled=True)  27.1 us
    all_to_all x2, starting transfers between devices, from_everyone(): lax.all_to_all(jnp.broadcast_to(array[None], (peers, *array.shape)), axis...  19.9 us
    all_to_all x2, waiting for transfers between devices, from_everyone(): lax.all_to_all(jnp.broadcast_to(array[None], (peers, *array.shape)), axis...  19.8 us
    dot_general x2, matrix products, on_device(): lax.dot_general(gathered, centres, (((0,), (0,)), ((), ())), preferred_el...  13.5 us
    all_to_all x1, starting transfers between devices, summed_on_arrival(): parts = lax.all_to_all(cut_along(array, dim, peers), axis, 0, 0, tiled=True)  10.6 us
  transfers between devices with their start and end apart: 7, of which 5 were waited for; matrix products, arithmetic and copies ran while one was open for 8% of the time, Pallas kernels for 0%

commit v1 on v0

--- a/solution.py
+++ b/solution.py
@@ -66,7 +66,13 @@
         chosen = local_picks[step]
         feats = jnp.take(pool, chosen, axis=1)
         labs = jnp.take(labels, chosen)
-        gathered = lax.all_gather(feats, "centre", axis=0, tiled=True)
+
+        def fill_tokens(chunk):
+            return jnp.concatenate(
+                lax.all_to_all(jnp.stack(lax.axis_size("centre") * [chunk]), "centre", 0, 0), axis=0
+            )
+
+        gathered = fill_tokens(feats)
         cross = lax.dot_general(
             gathered, centres, (((0,), (0,)), ((), ())), preferred_element_type=jnp.float32
         )

time: 337 us -> 392 us (1.16)
  waiting for transfers between devices: 176 us -> 221 us
  starting transfers between devices: 30.7 us -> 42.1 us
    all_to_all x0 -> x2, waiting for transfers between devices: none -> 53.1 us  [fill_tokens(): lax.all_to_all(jnp.stack(lax.axis_size('centre') * [chunk]), 'centre', 0, 0)]
    all_gather x2 -> x0, waiting for transfers between devices: 27.1 us -> none  [on_device(): gathered = lax.all_gather(feats, 'centre', axis=0, tiled=True)]
    all_to_all x2, waiting for transfers between devices: 19.8 us -> 42.9 us  [from_everyone(): lax.all_to_all(jnp.broadcast_to(array[None], (peers, *array.shape)), axis...]
    all_to_all x0 -> x2, starting transfers between devices: none -> 11.5 us  [fill_tokens(): lax.all_to_all(jnp.stack(lax.axis_size('centre') * [chunk]), 'centre', 0, 0)]
    all_gather x2, waiting for transfers between devices: 83.9 us -> 78.9 us  [over_pieces(): return lax.all_gather(array, axis).sum(0)]
  transfers between devices with their start and end apart: 7 -> 7, of which waited for: 5 -> 7; matrix products, arithmetic and copies ran while one was open for 8% -> 5% of each run, Pallas kernels for 0% -> 0%
where the time goes in v1:
time: 392 us; the launch traced here: 391 us
  waiting for transfers between devices  221 us (56%)
  blocking collectives  61.6 us (16%)
  starting transfers between devices  42.1 us (11%)
  local copies, waits for them, and re-layouts  20.9 us (5%)
  matrix products  20 us (5%)
  between operations  13.7 us (3%)
  other arithmetic  11.7 us (3%)
    all_gather x2, waiting for transfers between devices, over_pieces(): return lax.all_gather(array, axis).sum(0)  78.9 us
    all_to_all x1, blocking collectives, summed_on_arrival(): parts = lax.all_to_all(cut_along(array, dim, peers), axis, 0, 0, tiled=True)  61.6 us
    all_to_all x2, waiting for transfers between devices, fill_tokens(): lax.all_to_all(jnp.stack(lax.axis_size('centre') * [chunk]), 'centre', 0, 0)  53.1 us
    all_to_all x1, waiting for transfers between devices, summed_on_arrival(): parts = lax.all_to_all(cut_along(array, dim, peers), axis, 0, 0, tiled=True)  45.6 us
    all_to_all x2, waiting for transfers between devices, from_everyone(): lax.all_to_all(jnp.broadcast_to(array[None], (peers, *array.shape)), axis...  42.9 us
    all_to_all x2, starting transfers between devices, from_everyone(): lax.all_to_all(jnp.broadcast_to(array[None], (peers, *array.shape)), axis...  19.9 us
    all_to_all x2, starting transfers between devices, fill_tokens(): lax.all_to_all(jnp.stack(lax.axis_size('centre') * [chunk]), 'centre', 0, 0)  11.5 us
    dot_general x2, matrix products, on_device(): lax.dot_general(gathered, centres, (((0,), (0,)), ((), ())), preferred_el...  10.7 us
  transfers between devices with their start and end apart: 7, of which 7 were waited for; matrix products, arithmetic and copies ran while one was open for 5% of the time, Pallas kernels for 0%

profile of v1, /device:TPU:2, one launch (start us, length us, event | category | flops | bytes accessed | tf_op | source)
XLA Modules:
  0.0 390.6 jit_solution(17241617665069122735)
XLA Ops:
  7.3 2.3 gather_fusion.1
  10.7 1.3 gather_fusion
  12.3 1.1 stack.4
  13.4 7.2 %all-to-all-start = ((bf16[16,64,512]{2,1,0:T(8,128)(2,1)}), bf16[16,64,512]{2,1,0:T(8,128)(2,1)S(1)}, u32[]{:S(2)}, u32[]{:S(2)}) async-start(bf16[16,64,512]{2,1,0:T(8,128)(2,1)} %stack.4), calls=%async_computation | async-start | bytes 2097152 | tf_op jit(solution)/shard_map/all_to_all | solution.py:72
  20.6 26.6 %all-to-all-done = bf16[16,64,512]{2,1,0:T(8,128)(2,1)S(1)} async-done(((bf16[16,64,512]{2,1,0:T(8,128)(2,1)}), bf16[16,64,512]{2,1,0:T(8,128)(2,1)S(1)}, u32[]{:S(2)}, u32[]{:S(2)}) %all-to-all-start) | async-done | bytes 1048608 | tf_op jit(solution)/shard_map/all_to_all | solution.py:72
  47.3 1.2 broadcast_in_dim.19
  48.4 13.5 %all-to-all-start.1 = ((bf16[32,144,64]{1,2,0:T(8,128)(2,1)}), bf16[32,144,64]{1,2,0:T(8,128)(2,1)}, u32[]{:S(2)}, u32[]{:S(2)}) async-start(bf16[32,144,64]{1,2,0:T(8,128)(2,1)} %broadcast_in_dim.19), calls=%async_computation.1 | async-start | bytes 2097152 | tf_op jit(solution)/shard_map/all_to_all | solution.py:15
  62.0 3.2 multiply_reduce_fusion
  65.5 4.3 %exponential_convert_fusion.1 = bf16[512,2048]{1,0:T(8,128)(2,1)S(1)} fusion(bf16[1024,512]{1,0:T(8,128)(2,1)S(1)} %bitcast.35, bf16[1024,2048]{1,0:T(8,128)(2,1)S(1)} %copy-done.1, f32[2048]{0:T(1024)S(1)} %multiply_reduce_fusion, f32[512]{0:T(512)S(1)} %multiply_reduce_fusion.2), kind=kOutput, calls=%fused_computation.6 | convolution fusion | flops 2155872256 | bytes 7350272 | tf_op jit(solution)/shard_map/dot_general | solution.py:76
  69.8 20.9 %all-to-all-done.1 = bf16[32,144,64]{1,2,0:T(8,128)(2,1)} async-done(((bf16[32,144,64]{1,2,0:T(8,128)(2,1)}), bf16[32,144,64]{1,2,0:T(8,128)(2,1)}, u32[]{:S(2)}, u32[]{:S(2)}) %all-to-all-start.1) | async-done | bytes 589856 | tf_op jit(solution)/shard_map/all_to_all | solution.py:15
  90.7 2.8 convolution_bitcast_fusion
  93.5 39.5 %all-gather.5.cloned.1.call-done = f32[2304,512]{1,0:T(8,128)} async-done(((f32[144,512]{1,0:T(8,128)}), f32[2304,512]{1,0:T(8,128)}) %all-gather.5.cloned.1.call-update) | async-done | bytes 4718608 | tf_op jit(solution)/shard_map/all_gather | solution.py:32
  133.0 2.9 reduce_sum.83
  136.0 1.6 fusion.2
  137.5 2.1 reshape.45
  139.6 2.4 copy.47
  142.0 10.5 %all-to-all-start.2 = ((f32[32,144,64]{1,2,0:T(8,128)}), f32[32,144,64]{1,2,0:T(8,128)S(1)}, u32[]{:S(2)}, u32[]{:S(2)}) async-start(f32[32,144,64]{1,2,0:T(8,128)} %copy.47), calls=%async_computation.2 | async-start | bytes 4194304 | tf_op jit(solution)/shard_map/all_to_all | solution.py:43
  152.6 2.3 gather_fusion.3
  154.9 1.3 gather_fusion.2
  156.5 45.6 %all-to-all-done.2 = f32[32,144,64]{1,2,0:T(8,128)S(1)} async-done(((f32[32,144,64]{1,2,0:T(8,128)}), f32[32,144,64]{1,2,0:T(8,128)S(1)}, u32[]{:S(2)}, u32[]{:S(2)}) %all-to-all-start.2) | async-done | bytes 1179680 | tf_op jit(solution)/shard_map/all_to_all | solution.py:43
  203.2 4.3 %all-to-all-start.4 = ((bf16[16,64,512]{2,1,0:T(8,128)(2,1)}), bf16[16,64,512]{2,1,0:T(8,128)(2,1)S(1)}, u32[]{:S(2)}, u32[]{:S(2)}) async-start(bf16[16,64,512]{2,1,0:T(8,128)(2,1)} %stack.5), calls=%async_computation.4 | async-start | bytes 2097152 | tf_op jit(solution)/shard_map/all_to_all | solution.py:72
  207.7 26.5 %all-to-all-done.4 = bf16[16,64,512]{2,1,0:T(8,128)(2,1)S(1)} async-done(((bf16[16,64,512]{2,1,0:T(8,128)(2,1)}), bf16[16,64,512]{2,1,0:T(8,128)(2,1)S(1)}, u32[]{:S(2)}, u32[]{:S(2)}) %all-to-all-start.4) | async-done | bytes 1048608 | tf_op jit(solution)/shard_map/all_to_all | solution.py:72
  234.2 1.2 broadcast_in_dim.20
  235.4 6.4 %all-to-all-start.3 = ((bf16[32,144,64]{1,2,0:T(8,128)(2,1)}), bf16[32,144,64]{1,2,0:T(8,128)(2,1)}, u32[]{:S(2)}, u32[]{:S(2)}) async-start(bf16[32,144,64]{1,2,0:T(8,128)(2,1)} %broadcast_in_dim.20), calls=%async_computation.3 | async-start | bytes 2097152 | tf_op jit(solution)/shard_map/all_to_all | solution.py:15
  242.1 6.5 %exponential_convert_fusion = bf16[512,2048]{1,0:T(8,128)(2,1)S(1)} fusion(bf16[1024,512]{1,0:T(8,128)(2,1)S(1)} %bitcast.34, bf16[1024,2048]{1,0:T(8,128)(2,1)} %param.9, f32[512]{0:T(512)S(1)} %multiply_reduce_fusion.1, f32[2048]{0:T(1024)S(1)} %multiply_reduce_fusion), kind=kOutput, calls=%fused_computation.5 | convolution fusion | flops 2155872256 | bytes 7350272 | tf_op jit(solution)/shard_map/dot_general | solution.py:76
  248.6 22.0 %all-to-all-done.3 = bf16[32,144,64]{1,2,0:T(8,128)(2,1)} async-done(((bf16[32,144,64]{1,2,0:T(8,128)(2,1)}), bf16[32,144,64]{1,2,0:T(8,128)(2,1)}, u32[]{:S(2)}, u32[]{:S(2)}) %all-to-all-start.3) | async-done | bytes 589856 | tf_op jit(solution)/shard_map/all_to_all | solution.py:15
  270.6 2.8 fusion.16
  273.4 39.5 %all-gather.7.cloned.1.call-done = f32[2304,512]{1,0:T(8,128)} async-done(((f32[144,512]{1,0:T(8,128)}), f32[2304,512]{1,0:T(8,128)}) %all-gather.7.cloned.1.call-update) | async-done | bytes 4718608 | tf_op jit(solution)/shard_map/all_gather | solution.py:32
  312.9 2.9 reduce_sum.87
  315.9 2.1 fusion.3
  318.9 2.4 copy.53
  321.4 61.6 %all_to_all.30 = f32[32,144,64]{1,2,0:T(8,128)S(1)} all-to-all(f32[32,144,64]{1,2,0:T(8,128)} %copy.53), channel_id=1, replica_groups=mesh['centre'=16,'sample'=32] {'sample'}, dimensions={0} | all-to-all | bytes 2359296 | tf_op jit(solution)/shard_map/all_to_all | solution.py:43
  (44 shorter events, 6.2 us)
Async XLA Ops:
  6.5 0.8 copy-start
  6.5 14.1 %copy-start.5 = (f32[144,64]{0,1:T(8,128)S(1)}, f32[144,64]{0,1:T(8,128)}, u32[]{:S(2)}) copy-start(f32[144,64]{0,1:T(8,128)} %param.13) | copy-start | bytes 110596
  13.4 33.9 %all-to-all-start = ((bf16[16,64,512]{2,1,0:T(8,128)(2,1)}), bf16[16,64,512]{2,1,0:T(8,128)(2,1)S(1)}, u32[]{:S(2)}, u32[]{:S(2)}) async-start(bf16[16,64,512]{2,1,0:T(8,128)(2,1)} %stack.4), calls=%async_computation | async-start | bytes 2097152 | tf_op jit(solution)/shard_map/all_to_all | solution.py:72
  48.4 42.3 %all-to-all-start.1 = ((bf16[32,144,64]{1,2,0:T(8,128)(2,1)}), bf16[32,144,64]{1,2,0:T(8,128)(2,1)}, u32[]{:S(2)}, u32[]{:S(2)}) async-start(bf16[32,144,64]{1,2,0:T(8,128)(2,1)} %broadcast_in_dim.19), calls=%async_computation.1 | async-start | bytes 2097152 | tf_op jit(solution)/shard_map/all_to_all | solution.py:15
  61.9 71.1 %all-gather.5.cloned.1.call-start = ((), (), s32[]{:S(2)}) async-start(), calls=%async_computation.6 | async-start | bytes 5013504 | tf_op jit(solution)/shard_map/all_gather | solution.py:32
  62.0 3.5 copy-start.1
  142.0 60.1 %all-to-all-start.2 = ((f32[32,144,64]{1,2,0:T(8,128)}), f32[32,144,64]{1,2,0:T(8,128)S(1)}, u32[]{:S(2)}, u32[]{:S(2)}) async-start(f32[32,144,64]{1,2,0:T(8,128)} %copy.47), calls=%async_computation.2 | async-start | bytes 4194304 | tf_op jit(solution)/shard_map/all_to_all | solution.py:43
  203.2 31.0 %all-to-all-start.4 = ((bf16[16,64,512]{2,1,0:T(8,128)(2,1)}), bf16[16,64,512]{2,1,0:T(8,128)(2,1)S(1)}, u32[]{:S(2)}, u32[]{:S(2)}) async-start(bf16[16,64,512]{2,1,0:T(8,128)(2,1)} %stack.5), calls=%async_computation.4 | async-start | bytes 2097152 | tf_op jit(solution)/shard_map/all_to_all | solution.py:72
  207.7 34.4 %copy-start.3 = (f32[144,64]{0,1:T(8,128)}, f32[144,64]{0,1:T(8,128)S(1)}, u32[]{:S(2)}) copy-start(f32[144,64]{0,1:T(8,128)S(1)} %reduce_sum.85) | copy-start | bytes 110596
  235.4 35.2 %all-to-all-start.3 = ((bf16[32,144,64]{1,2,0:T(8,128)(2,1)}), bf16[32,144,64]{1,2,0:T(8,128)(2,1)}, u32[]{:S(2)}, u32[]{:S(2)}) async-start(bf16[32,144,64]{1,2,0:T(8,128)(2,1)} %broadcast_in_dim.20), calls=%async_computation.3 | async-start | bytes 2097152 | tf_op jit(solution)/shard_map/all_to_all | solution.py:15
  241.8 71.1 %all-gather.7.cloned.1.call-start = ((), (), s32[]{:S(2)}) async-start(), calls=%async_computation.7 | async-start | bytes 5013504 | tf_op jit(solution)/shard_map/all_gather | solution.py:32
  248.6 64.3 %copy-start.2 = (bf16[512,2048]{1,0:T(8,128)(2,1)}, bf16[512,2048]{1,0:T(8,128)(2,1)S(1)}, u32[]{:S(2)}) copy-start(bf16[512,2048]{1,0:T(8,128)(2,1)S(1)} %exponential_convert_fusion) | copy-start | bytes 6291460
  321.4 61.7 %copy-start.4 = (f32[144,64]{0,1:T(8,128)S(1)}, f32[144,64]{0,1:T(8,128)}, u32[]{:S(2)}) copy-start(f32[144,64]{0,1:T(8,128)} %copy-done.3) | copy-start | bytes 110596
  321.4 61.7 %copy-start.6 = (f32[144,64]{0,1:T(8,128)S(1)}, f32[144,64]{0,1:T(8,128)}, u32[]{:S(2)}) copy-start(f32[144,64]{0,1:T(8,128)} %param.13) | copy-start | bytes 110596
Sparse Core Ops, SparseCore 0:
  93.6 39.3 all-gather.4
  273.5 39.3 all-gather.6
